TPU v7x, 32 devices: a whole 2x2x4 slice. The times are simulated.
32 devices in a mesh: fsdp: 2 (over x), context: 4 (over z), tensor: 4 (over y, core).
Axes of the slice: x: 2, y: 2, z: 4, core: 2. Of those that a mesh axis runs over, the one named last changes fastest.
Arguments:
- inputs: bfloat16 [4096, 1536], P(('fsdp', 'context')), may hold values from -6 to 6
- cotangent: bfloat16 [4096, 1536], P(('fsdp', 'context')), may hold values from -6 to 6
- blocks: int32 [2, 8], P('fsdp'), may hold values from 0 to 7, each once within a row
- attn_gain: bfloat16 [1536], P('fsdp'), may hold values from 0.25 to 1.75
- w_query: bfloat16 [1536, 1536], P('fsdp', 'tensor'), may hold values from -0.21875 to 0.21875
- b_query: bfloat16 [12, 128], P('tensor', 'fsdp'), may hold values from -3 to 3
- w_key: bfloat16 [1536, 256], P('fsdp'), may hold values from -0.21875 to 0.21875
- b_key: bfloat16 [2, 128], P(None, 'fsdp'), may hold values from -3 to 3
- w_value: bfloat16 [1536, 256], P('fsdp'), may hold values from -0.15625 to 0.15625
- b_value: bfloat16 [2, 128], P(None, 'fsdp'), may hold values from -3 to 3
- w_out: bfloat16 [1536, 1536], P('tensor', 'fsdp'), may hold values from -1 to 1
- ffn_gain: bfloat16 [1536], P('fsdp'), may hold values from 0.25 to 1.75
- w_gate: bfloat16 [1536, 8960], P('fsdp', 'tensor'), may hold values from -0.15625 to 0.15625
- w_up: bfloat16 [1536, 8960], P('fsdp', 'tensor'), may hold values from -0.15625 to 0.15625
- w_down: bfloat16 [8960, 1536], P('tensor', 'fsdp'), may hold values from -0.09375 to 0.09375
Outputs:
- outputs: bfloat16 [4096, 1536], P(('fsdp', 'context'))
- input_grad: bfloat16 [4096, 1536], P(('fsdp', 'context'))
- attn_gain_grad: float32 [1536], P('fsdp')
- w_query_grad: float32 [1536, 1536], P('fsdp', 'tensor')
- b_query_grad: float32 [12, 128], P('tensor', 'fsdp')
- w_key_grad: float32 [1536, 256], P('fsdp')
- b_key_grad: float32 [2, 128], P(None, 'fsdp')
- w_value_grad: float32 [1536, 256], P('fsdp')
- b_value_grad: float32 [2, 128], P(None, 'fsdp')
- w_out_grad: float32 [1536, 1536], P('tensor', 'fsdp')
- ffn_gain_grad: float32 [1536], P('fsdp')
- w_gate_grad: float32 [1536, 8960], P('fsdp', 'tensor')
- w_up_grad: float32 [1536, 8960], P('fsdp', 'tensor')
- w_down_grad: float32 [8960, 1536], P('tensor', 'fsdp')
Inputs may be any that keep to these rules, and one draw needn't show every extreme that they name: `blocks`: each row lists every block number of 0 to 7 once.
All inputs are finite; a program needn't handle non-finite values.
Results may differ from a plain program's by a relative error of at most 0.02.
Values may be sent and summed in bfloat16 or wider, within the bound.
A program may use at most 192 MiB of HBM per device.

v0:
```python
import jax
import jax.numpy as jnp
from jax import lax
from jax.sharding import PartitionSpec as P

H = 12
KV = 2
HD = 128
BLOCK = 256
EPSILON = 1e-06
ROPE_BASE = 1000000.0
MASKED = -1e30


def rope_tables(positions):
    halfway = HD // 2
    frequency = ROPE_BASE ** (-(jnp.arange(halfway, dtype=jnp.float32) * 2.0 / HD))
    angles = positions.astype(jnp.float32)[:, None] * frequency[None, :]
    cosine = jnp.concatenate([jnp.cos(angles), jnp.cos(angles)], axis=1)
    sine = jnp.concatenate([jnp.sin(angles), jnp.sin(angles)], axis=1)
    return (cosine, sine)


def rotate(field, cosine, sine):
    halfway = HD // 2
    turned = jnp.concatenate([-field[..., halfway:], field[..., :halfway]], axis=-1)
    return field * cosine[:, None, :] + turned * sine[:, None, :]


def rotate_back(grad_field, cosine, sine):
    halfway = HD // 2
    moved = grad_field * sine[:, None, :]
    turned = jnp.concatenate([moved[..., halfway:], -moved[..., :halfway]], axis=-1)
    return grad_field * cosine[:, None, :] + turned


def rms_scale(values):
    return lax.rsqrt(jnp.mean(values * values, axis=-1, keepdims=True) + EPSILON)


def norm_back(values, factor, gain, grad_normed):
    gained = gain * grad_normed
    inner = jnp.mean(gained * values, axis=-1, keepdims=True)
    grad_values = factor * gained - values * (factor * factor * factor) * inner
    return (grad_values, jnp.sum(grad_normed * values * factor, axis=0))


def contract_rows(left, right):
    return lax.dot_general(
        left, right, (((0,), (0,)), ((), ())), preferred_element_type=jnp.float32
    )


def contract_cols(left, right):
    return lax.dot_general(
        left, right, (((1,), (1,)), ((), ())), preferred_element_type=jnp.float32
    )


def local(
    inputs,
    cotangent,
    blocks,
    attn_gain,
    w_query,
    b_query,
    w_key,
    b_key,
    w_value,
    b_value,
    w_out,
    ffn_gain,
    w_gate,
    w_up,
    w_down,
):
    rows_here = inputs.shape[0]
    context_index = lax.axis_index("context")
    tensor_index = lax.axis_index("tensor")
    gain_first, wq_all, bq_all, wk_all, bk_all, wv_all, bv_all, wo_all = (
        lax.all_gather(attn_gain, "fsdp", axis=0, tiled=True),
        lax.all_gather(w_query, "fsdp", axis=0, tiled=True),
        lax.all_gather(b_query, "fsdp", axis=1, tiled=True),
        lax.all_gather(w_key, "fsdp", axis=0, tiled=True),
        lax.all_gather(b_key, "fsdp", axis=1, tiled=True),
        lax.all_gather(w_value, "fsdp", axis=0, tiled=True),
        lax.all_gather(b_value, "fsdp", axis=1, tiled=True),
        lax.all_gather(w_out, "fsdp", axis=1, tiled=True),
    )
    seq_blocks = blocks[0]
    seq_length = seq_blocks.shape[0] * BLOCK
    block_of_row = jnp.repeat(seq_blocks, BLOCK, total_repeat_length=seq_length)
    key_positions = block_of_row * BLOCK + jnp.arange(seq_length, dtype=jnp.int32) % BLOCK
    my_blocks = lax.dynamic_slice_in_dim(block_of_row, context_index * rows_here, rows_here)
    my_positions = lax.dynamic_slice_in_dim(key_positions, context_index * rows_here, rows_here)
    cosine, sine = rope_tables(my_positions)
    allowed = block_of_row[None, :] <= my_blocks[:, None]
    inputs_f = inputs.astype(jnp.float32)
    factor_first = rms_scale(inputs_f)
    gain_first_f = gain_first.astype(jnp.float32)
    normed = (inputs_f * factor_first * gain_first_f).astype(jnp.bfloat16)
    query_pre = jnp.dot(normed, wq_all, preferred_element_type=jnp.float32).reshape(
        rows_here, -1, HD
    ) + bq_all.astype(jnp.float32)
    key_pre = jnp.dot(normed, wk_all, preferred_element_type=jnp.float32).reshape(
        rows_here, KV, HD
    ) + bk_all.astype(jnp.float32)
    value_pre = jnp.dot(normed, wv_all, preferred_element_type=jnp.float32).reshape(
        rows_here, KV, HD
    ) + bv_all.astype(jnp.float32)
    queries = rotate(query_pre, cosine, sine).astype(jnp.bfloat16)
    keys = rotate(key_pre, cosine, sine).astype(jnp.bfloat16)
    values = value_pre.astype(jnp.bfloat16)
    key_whole, value_whole = (
        lax.all_gather(keys, "context", axis=0, tiled=True),
        lax.all_gather(values, "context", axis=0, tiled=True),
    )
    heads_here = queries.shape[1]
    group_size = H // KV
    scaling = HD ** (-0.5)
    attended_list = []
    log_totals = []
    for head_slot in range(heads_here):
        key_group = (tensor_index * heads_here + head_slot) // group_size
        key_head = lax.dynamic_index_in_dim(key_whole, key_group, 1, keepdims=False)
        value_head = lax.dynamic_index_in_dim(value_whole, key_group, 1, keepdims=False)
        raw_scores = (
            jnp.einsum(
                "qd,kd->qk", queries[:, head_slot], key_head, preferred_element_type=jnp.float32
            )
            * scaling
        )
        scores = jnp.where(allowed, raw_scores, MASKED)
        row_max = jnp.max(scores, axis=1, keepdims=True)
        expo = jnp.exp(scores - row_max)
        total = jnp.sum(expo, axis=1, keepdims=True)
        probability = (expo / total).astype(jnp.bfloat16)
        attended_list.append(jnp.dot(probability, value_head, preferred_element_type=jnp.float32))
        log_totals.append(row_max + jnp.log(total))
    attended = jnp.concatenate(attended_list, axis=1).astype(jnp.bfloat16)
    attn_part = jnp.dot(attended, wo_all, preferred_element_type=jnp.float32)
    middle = inputs_f + lax.psum(attn_part, "tensor")
    gain_second, wg_all, wu_all, wd_all = (
        lax.all_gather(ffn_gain, "fsdp", axis=0, tiled=True),
        lax.all_gather(w_gate, "fsdp", axis=0, tiled=True),
        lax.all_gather(w_up, "fsdp", axis=0, tiled=True),
        lax.all_gather(w_down, "fsdp", axis=1, tiled=True),
    )
    factor_second = rms_scale(middle)
    gain_second_f = gain_second.astype(jnp.float32)
    normed2 = (middle * factor_second * gain_second_f).astype(jnp.bfloat16)
    gate_pre = jnp.dot(normed2, wg_all, preferred_element_type=jnp.float32)
    up_pre = jnp.dot(normed2, wu_all, preferred_element_type=jnp.float32)
    sigma = jax.nn.sigmoid(gate_pre)
    hidden = (gate_pre * sigma * up_pre).astype(jnp.bfloat16)
    ffn_part = jnp.dot(hidden, wd_all, preferred_element_type=jnp.float32)
    final = middle + lax.psum(ffn_part.astype(jnp.bfloat16), "tensor").astype(jnp.float32)
    outputs = final.astype(jnp.bfloat16)
    grad_out = cotangent.astype(jnp.float32)
    wd_grad = contract_rows(hidden, cotangent)
    grad_hidden = contract_cols(cotangent, wd_all)
    grad_gate = (grad_hidden * up_pre * (sigma + gate_pre * sigma * (1.0 - sigma))).astype(
        jnp.bfloat16
    )
    grad_upper = (grad_hidden * gate_pre * sigma).astype(jnp.bfloat16)
    wg_grad = contract_rows(normed2, grad_gate)
    wu_grad = contract_rows(normed2, grad_upper)
    normed2_part = contract_cols(grad_gate, wg_all) + contract_cols(grad_upper, wu_all)
    grad_normed2 = lax.psum(normed2_part, "tensor")
    grad_mid_norm, ffn_gain_grad = norm_back(middle, factor_second, gain_second_f, grad_normed2)
    grad_middle = grad_out + grad_mid_norm
    grad_middle_low = grad_middle.astype(jnp.bfloat16)
    wo_grad = contract_rows(attended, grad_middle_low)
    grad_attended = contract_cols(grad_middle_low, wo_all).astype(jnp.bfloat16)
    key_grad = jnp.zeros((seq_length, KV, HD), jnp.float32)
    value_grad = jnp.zeros((seq_length, KV, HD), jnp.float32)
    query_grads = []
    for head_slot in range(heads_here):
        key_group = (tensor_index * heads_here + head_slot) // group_size
        key_head = lax.dynamic_index_in_dim(key_whole, key_group, 1, keepdims=False)
        value_head = lax.dynamic_index_in_dim(value_whole, key_group, 1, keepdims=False)
        query_head = queries[:, head_slot]
        raw_scores = (
            jnp.einsum("qd,kd->qk", query_head, key_head, preferred_element_type=jnp.float32)
            * scaling
        )
        scores = jnp.where(allowed, raw_scores, MASKED)
        probability = jnp.exp(scores - log_totals[head_slot])
        prob_low = probability.astype(jnp.bfloat16)
        grad_head = grad_attended[:, head_slot * HD : (head_slot + 1) * HD]
        grad_probs = jnp.einsum(
            "qd,kd->qk", grad_head, value_head, preferred_element_type=jnp.float32
        )
        inner = jnp.sum(probability * grad_probs, axis=1, keepdims=True)
        grad_scores = (probability * (grad_probs - inner)).astype(jnp.bfloat16)
        query_grads.append(
            jnp.dot(grad_scores, key_head, preferred_element_type=jnp.float32) * scaling
        )
        key_piece = contract_rows(grad_scores, query_head) * scaling
        value_piece = contract_rows(prob_low, grad_head)
        select = (jnp.arange(KV, dtype=jnp.int32) == key_group)[None, :, None]
        key_grad = key_grad + jnp.where(select, key_piece[:, None, :], 0.0)
        value_grad = value_grad + jnp.where(select, value_piece[:, None, :], 0.0)
    key_share, value_share = (
        lax.psum_scatter(key_grad, "context", scatter_dimension=0, tiled=True),
        lax.psum_scatter(value_grad, "context", scatter_dimension=0, tiled=True),
    )
    query_grad = jnp.stack(query_grads, axis=1)
    query_low = rotate_back(query_grad, cosine, sine).astype(jnp.bfloat16)
    flat_query = query_low.reshape(rows_here, -1)
    normed_part = contract_cols(flat_query, wq_all)
    grad_normed_query, key_total, value_total = lax.psum(
        (normed_part, key_share, value_share), "tensor"
    )
    key_low = rotate_back(key_total, cosine, sine).astype(jnp.bfloat16)
    value_low = value_total.astype(jnp.bfloat16)
    flat_key = key_low.reshape(rows_here, -1)
    flat_value = value_low.reshape(rows_here, -1)
    grad_normed = (
        grad_normed_query + contract_cols(flat_key, wk_all) + contract_cols(flat_value, wv_all)
    )
    grad_in_norm, attn_gain_grad = norm_back(inputs_f, factor_first, gain_first_f, grad_normed)
    input_grad = (grad_middle + grad_in_norm).astype(jnp.bfloat16)
    wq_grad = contract_rows(normed, flat_query)
    bq_grad = jnp.sum(query_low.astype(jnp.float32), axis=0)
    wk_grad = contract_rows(normed, flat_key)
    bk_grad = jnp.sum(key_low.astype(jnp.float32), axis=0)
    wv_grad = contract_rows(normed, flat_value)
    bv_grad = jnp.sum(value_low.astype(jnp.float32), axis=0)
    pieces = (
        lax.psum_scatter(
            attn_gain_grad.astype(jnp.bfloat16),
            ("fsdp", "context"),
            scatter_dimension=0,
            tiled=True,
        ).astype(jnp.float32),
        lax.psum_scatter(
            wq_grad.astype(jnp.bfloat16), ("fsdp", "context"), scatter_dimension=0, tiled=True
        ).astype(jnp.float32),
        lax.psum_scatter(
            bq_grad.astype(jnp.bfloat16), ("fsdp", "context"), scatter_dimension=1, tiled=True
        ).astype(jnp.float32),
        lax.psum_scatter(
            wk_grad.astype(jnp.bfloat16), ("fsdp", "context"), scatter_dimension=0, tiled=True
        ).astype(jnp.float32),
        lax.psum_scatter(
            bk_grad.astype(jnp.bfloat16), ("fsdp", "context"), scatter_dimension=1, tiled=True
        ).astype(jnp.float32),
        lax.psum_scatter(
            wv_grad.astype(jnp.bfloat16), ("fsdp", "context"), scatter_dimension=0, tiled=True
        ).astype(jnp.float32),
        lax.psum_scatter(
            bv_grad.astype(jnp.bfloat16), ("fsdp", "context"), scatter_dimension=1, tiled=True
        ).astype(jnp.float32),
        lax.psum_scatter(
            wo_grad.astype(jnp.bfloat16), ("fsdp", "context"), scatter_dimension=1, tiled=True
        ).astype(jnp.float32),
        lax.psum_scatter(
            ffn_gain_grad.astype(jnp.bfloat16), ("fsdp", "context"), scatter_dimension=0, tiled=True
        ).astype(jnp.float32),
        lax.psum_scatter(
            wg_grad.astype(jnp.bfloat16), ("fsdp", "context"), scatter_dimension=0, tiled=True
        ).astype(jnp.float32),
        lax.psum_scatter(
            wu_grad.astype(jnp.bfloat16), ("fsdp", "context"), scatter_dimension=0, tiled=True
        ).astype(jnp.float32),
        lax.psum_scatter(
            wd_grad.astype(jnp.bfloat16), ("fsdp", "context"), scatter_dimension=1, tiled=True
        ).astype(jnp.float32),
    )
    shards = (
        lax.all_gather(pieces[0].astype(jnp.bfloat16), "context", axis=0, tiled=True).astype(
            jnp.float32
        ),
        lax.all_gather(pieces[1].astype(jnp.bfloat16), "context", axis=0, tiled=True).astype(
            jnp.float32
        ),
        lax.all_gather(pieces[2].astype(jnp.bfloat16), "context", axis=1, tiled=True).astype(
            jnp.float32
        ),
        lax.all_gather(pieces[3].astype(jnp.bfloat16), "context", axis=0, tiled=True).astype(
            jnp.float32
        ),
        lax.all_gather(pieces[4].astype(jnp.bfloat16), "context", axis=1, tiled=True).astype(
            jnp.float32
        ),
        lax.all_gather(pieces[5].astype(jnp.bfloat16), "context", axis=0, tiled=True).astype(
            jnp.float32
        ),
        lax.all_gather(pieces[6].astype(jnp.bfloat16), "context", axis=1, tiled=True).astype(
            jnp.float32
        ),
        lax.all_gather(pieces[7].astype(jnp.bfloat16), "context", axis=1, tiled=True).astype(
            jnp.float32
        ),
        lax.all_gather(pieces[8].astype(jnp.bfloat16), "context", axis=0, tiled=True).astype(
            jnp.float32
        ),
        lax.all_gather(pieces[9].astype(jnp.bfloat16), "context", axis=0, tiled=True).astype(
            jnp.float32
        ),
        lax.all_gather(pieces[10].astype(jnp.bfloat16), "context", axis=0, tiled=True).astype(
            jnp.float32
        ),
        lax.all_gather(pieces[11].astype(jnp.bfloat16), "context", axis=1, tiled=True).astype(
            jnp.float32
        ),
    )
    return (
        outputs,
        input_grad,
        shards[0],
        shards[1],
        shards[2],
        shards[3],
        shards[4],
        shards[5],
        shards[6],
        shards[7],
        shards[8],
        shards[9],
        shards[10],
        shards[11],
    )


def solution(mesh):
    in_specs = (
        P(("fsdp", "context"), None),
        P(("fsdp", "context"), None),
        P("fsdp", None),
        P("fsdp"),
        P("fsdp", "tensor"),
        P("tensor", "fsdp"),
        P("fsdp", None),
        P(None, "fsdp"),
        P("fsdp", None),
        P(None, "fsdp"),
        P("tensor", "fsdp"),
        P("fsdp"),
        P("fsdp", "tensor"),
        P("fsdp", "tensor"),
        P("tensor", "fsdp"),
    )
    out_specs = (
        P(("fsdp", "context"), None),
        P(("fsdp", "context"), None),
        P("fsdp"),
        P("fsdp", "tensor"),
        P("tensor", "fsdp"),
        P("fsdp", None),
        P(None, "fsdp"),
        P("fsdp", None),
        P(None, "fsdp"),
        P("tensor", "fsdp"),
        P("fsdp"),
        P("fsdp", "tensor"),
        P("fsdp", "tensor"),
        P("tensor", "fsdp"),
    )
    return jax.shard_map(local, mesh=mesh, in_specs=in_specs, out_specs=out_specs, check_vma=False)
```

profile of v0, /device:TPU:0, one launch (start us, length us, event | category | flops | bytes accessed | tf_op | source)
XLA Modules:
  0.0 1892.9 jit_solution(14799244396280470210)
XLA Ops:
  11.2 5.2 all-gather
  17.9 19.9 %all_gather.81 = bf16[1536,256]{1,0:T(8,128)(2,1)S(1)} all-gather(bf16[768,256]{1,0:T(8,128)(2,1)} %param.23), channel_id=1, replica_groups=mesh['fsdp'=2,'context'=4,'tensor'=4] {'fsdp'}, dimensions={0}, use_global_device_ids=true | all-gather | bytes 1179648 | tf_op jit(solution)/shard_map/all_gather | solution.py:84
  37.9 5.2 select_select_fusion
  43.8 4.5 all-gather.2
  50.4 4.2 all-gather.3
  54.7 8.8 all_gather.84
  65.8 4.5 all-gather.1
  73.1 7.2 all-gather.21.cloned.1.call-done
  92.5 17.4 all-gather.23.cloned.1.call-done
  109.9 3.5 fusion.32
  117.1 16.5 all-gather.25.cloned.1.call-done
  133.6 3.9 fusion.71
  139.7 4.9 all-gather.4
  144.6 61.5 %all-reduce.13.cloned.1.call-done = f32[512,1536]{1,0:T(8,128)} async-done(((f32[512,1536]{1,0:T(8,128)}), f32[512,1536]{1,0:T(8,128)}) %all-reduce.13.cloned.1.call-update) | async-done | bytes 3145744 | tf_op jit(solution)/shard_map/psum | solution.py:142
  212.0 82.6 %all-gather.29.cloned.1.call-done = bf16[1536,2240]{0,1:T(8,128)(2,1)} async-done(((bf16[768,2240]{0,1:T(8,128)(2,1)}), bf16[1536,2240]{0,1:T(8,128)(2,1)}) %all-gather.29.cloned.1.call-update) | async-done | bytes 6881296 | tf_op jit(solution)/shard_map/all_gather | solution.py:146
  294.7 9.5 fusion.117
  304.2 79.1 %all-gather.27.cloned.1.call-done = bf16[1536,2240]{0,1:T(8,128)(2,1)} async-done(((bf16[768,2240]{0,1:T(8,128)(2,1)}), bf16[1536,2240]{0,1:T(8,128)(2,1)}) %all-gather.27.cloned.1.call-update) | async-done | bytes 6881296 | tf_op jit(solution)/shard_map/all_gather | solution.py:145
  383.3 9.5 fusion.116
  392.8 79.1 %all-gather.31.cloned.1.call-done = bf16[2240,1536]{1,0:T(8,128)(2,1)} async-done(((bf16[2240,768]{1,0:T(8,128)(2,1)}), bf16[2240,1536]{1,0:T(8,128)(2,1)}) %all-gather.31.cloned.1.call-update) | async-done | bytes 6881296 | tf_op jit(solution)/shard_map/all_gather | solution.py:147
  471.9 13.3 multiply_convert_fusion
  485.2 4.0 fusion.118
  489.2 8.6 convolution_add_fusion.2
  500.2 9.1 convolution_convert_fusion.3
  510.3 56.2 %all-reduce.17.cloned.1.call-done = f32[512,1536]{1,0:T(8,128)} async-done(((f32[512,1536]{1,0:T(8,128)}), f32[512,1536]{1,0:T(8,128)}) %all-reduce.17.cloned.1.call-update) | async-done | bytes 3145744 | tf_op jit(solution)/shard_map/psum | solution.py:169
  566.4 3.3 multiply_reduce_fusion.3
  570.3 41.9 %all-reduce.15.cloned.1.call-done = bf16[512,1536]{1,0:T(8,128)(2,1)} async-done(((bf16[512,1536]{1,0:T(8,128)(2,1)}), bf16[512,1536]{1,0:T(8,128)(2,1)}) %all-reduce.15.cloned.1.call-update) | async-done | bytes 1572880 | tf_op jit(solution)/shard_map/psum | solution.py:157
  612.2 6.0 subtract_add_fusion
  636.1 3.5 multiply_reduce_fusion.1
  647.2 3.5 multiply_reduce_fusion.2
  658.8 6.0 select_add_fusion
  675.0 34.0 %reduce-scatter.19.cloned.1.call-done = f32[512,2,128]{0,2,1:T(8,128)} async-done(((f32[2048,2,128]{0,2,1:T(8,128)}), f32[512,2,128]{0,2,1:T(8,128)}) %reduce-scatter.19.cloned.1.call-update) | async-done | bytes 524304 | tf_op jit(solution)/shard_map/reduce_scatter | solution.py:205
  709.1 8.8 convolution_convert_fusion
  718.1 9.0 convolution_convert_fusion.2
  727.2 8.9 convolution_convert_fusion.1
  740.1 3.7 convolution_convert_fusion.5
  743.8 10.6 reduce-scatter.21.cloned.1.call-done
  754.5 23.9 %all-reduce.20 = bf16[512,2,128]{0,2,1:T(8,128)(2,1)} all-reduce(f32[512,2,128]{0,2,1:T(8,128)} %reduce-scatter.21.cloned.1.call-done), channel_id=1, replica_groups=mesh['fsdp'=2,'context'=4,'tensor'=4] {'tensor'}, use_global_device_ids=true, to_apply=%region_19.20 | all-reduce | flops 131072 | bytes 786432 | tf_op jit(solution)/shard_map/psum | solution.py:212
  780.2 3.1 convolution_convert_fusion.6
  783.4 54.8 %all-reduce.19.cloned.1.call-done = (f32[512,1536]{1,0:T(8,128)}, f32[512,2,128]{0,2,1:T(8,128)}) async-done(((f32[512,1536]{1,0:T(8,128)}, f32[512,2,128]{0,2,1:T(8,128)}), (f32[512,1536]{1,0:T(8,128)}, f32[512,2,128]{0,2,1:T(8,128)})) %all-reduce.19.cloned.1.call-update) | async-done | bytes 3670032 | tf_op jit(solution)/shard_map/psum | solution.py:212
  844.9 126.1 %reduce-scatter.35.cloned.1.call-done = bf16[2240,192]{0,1:T(8,128)(2,1)} async-done(((bf16[2240,1536]{0,1:T(8,128)(2,1)}), bf16[2240,192]{0,1:T(8,128)(2,1)}) %reduce-scatter.35.cloned.1.call-update) | async-done | bytes 860176 | tf_op jit(solution)/shard_map/reduce_scatter | solution.py:267
  971.0 132.0 %reduce-scatter.31.cloned.1.call-done = bf16[192,2240]{1,0:T(8,128)(2,1)} async-done(((bf16[1536,2240]{1,0:T(8,128)(2,1)}), bf16[192,2240]{1,0:T(8,128)(2,1)}) %reduce-scatter.31.cloned.1.call-update) | async-done | bytes 860176 | tf_op jit(solution)/shard_map/reduce_scatter | solution.py:261
  1103.1 131.5 %reduce-scatter.33.cloned.1.call-done = bf16[192,2240]{1,0:T(8,128)(2,1)} async-done(((bf16[1536,2240]{1,0:T(8,128)(2,1)}), bf16[192,2240]{1,0:T(8,128)(2,1)}) %reduce-scatter.33.cloned.1.call-update) | async-done | bytes 860176 | tf_op jit(solution)/shard_map/reduce_scatter | solution.py:264
  1237.1 53.9 %reduce-scatter.37.cloned.1.call-done = bf16[16,3]{1,0:T(8,128)(2,1)} async-done(((bf16[128,3]{1,0:T(8,128)(2,1)}), bf16[16,3]{1,0:T(8,128)(2,1)}) %reduce-scatter.37.cloned.1.call-update) | async-done | bytes 112
  1291.8 9.9 all-gather.5
  1302.4 56.1 %reduce-scatter.29.cloned.1.call-done = bf16[384,192]{0,1:T(8,128)(2,1)} async-done(((bf16[384,1536]{0,1:T(8,128)(2,1)}), bf16[384,192]{0,1:T(8,128)(2,1)}) %reduce-scatter.29.cloned.1.call-update) | async-done | bytes 147472 | tf_op jit(solution)/shard_map/reduce_scatter | solution.py:255
  1358.5 17.8 all_gather.99
  1378.6 47.2 %reduce-scatter.23.cloned.1.call-done = bf16[192,384]{1,0:T(8,128)(2,1)} async-done(((bf16[1536,384]{1,0:T(8,128)(2,1)}), bf16[192,384]{1,0:T(8,128)(2,1)}) %reduce-scatter.23.cloned.1.call-update) | async-done | bytes 147472 | tf_op jit(solution)/shard_map/reduce_scatter | solution.py:237
  1425.8 16.7 all_gather.93
  1443.6 38.0 %reduce-scatter.41.cloned.1.call-done = bf16[16,2]{1,0:T(8,128)(2,1)} async-done(((bf16[128,2]{1,0:T(8,128)(2,1)}), bf16[16,2]{1,0:T(8,128)(2,1)}) %reduce-scatter.41.cloned.1.call-update) | async-done | bytes 80
  1482.3 9.8 all-gather.7
  1492.8 54.5 %reduce-scatter.27.cloned.1.call-done = bf16[192,256]{1,0:T(8,128)(2,1)} async-done(((bf16[1536,256]{1,0:T(8,128)(2,1)}), bf16[192,256]{1,0:T(8,128)(2,1)}) %reduce-scatter.27.cloned.1.call-update) | async-done | bytes 98320 | tf_op jit(solution)/shard_map/reduce_scatter | solution.py:249
  1547.4 15.3 all_gather.97
  1569.5 20.2 %all-reduce.5 = (bf16[1536]{0:T(1024)(128)(2,1)S(1)}, bf16[1536]{0:T(1024)(128)(2,1)S(1)}) all-reduce(bf16[1536]{0:T(1024)(128)(2,1)S(1)} %get-tuple-element.84, bf16[1536]{0:T(1024)(128)(2,1)S(1)} %copy-done.40), channel_id=4, replica_groups=mesh['fsdp'=2,'context'=4,'tensor'=4] {'fsdp','context'}, use_global_device_ids=true, to_apply=%region_22.23.clone | all-reduce | flops 3072 | bytes 12288
  1590.3 8.3 all-reduce.6
  1599.8 4.3 fusion.12
  1604.9 9.5 all-gather.6
  1615.1 53.3 %reduce-scatter.25.cloned.1.call-done = bf16[192,256]{1,0:T(8,128)(2,1)} async-done(((bf16[1536,256]{1,0:T(8,128)(2,1)}), bf16[192,256]{1,0:T(8,128)(2,1)}) %reduce-scatter.25.cloned.1.call-update) | async-done | bytes 98320 | tf_op jit(solution)/shard_map/reduce_scatter | solution.py:243
  1668.4 16.2 all_gather.95
  1685.5 54.4 %all-gather.37.cloned.1.call-done = bf16[2240,768]{0,1:T(8,128)(2,1)} async-done(((bf16[2240,192]{0,1:T(8,128)(2,1)}), bf16[2240,768]{0,1:T(8,128)(2,1)}) %all-gather.37.cloned.1.call-update) | async-done | bytes 3440656 | tf_op jit(solution)/shard_map/all_gather | solution.py:305
  1739.9 5.9 copy.88
  1745.8 64.4 %all-gather.33.cloned.1.call-done = bf16[768,2240]{1,0:T(8,128)(2,1)} async-done(((bf16[192,2240]{1,0:T(8,128)(2,1)}), bf16[768,2240]{1,0:T(8,128)(2,1)}) %all-gather.33.cloned.1.call-update) | async-done | bytes 3440656 | tf_op jit(solution)/shard_map/all_gather | solution.py:299
  1810.2 5.9 copy.86
  1816.0 64.3 %all-gather.35.cloned.1.call-done = bf16[768,2240]{1,0:T(8,128)(2,1)} async-done(((bf16[192,2240]{1,0:T(8,128)(2,1)}), bf16[768,2240]{1,0:T(8,128)(2,1)}) %all-gather.35.cloned.1.call-update) | async-done | bytes 3440656 | tf_op jit(solution)/shard_map/all_gather | solution.py:302
  1880.3 5.9 copy.87
  (288 shorter events, 115.5 us)
Async XLA Ops:
  7.2 30.7 %copy-start.49 = (pred[2048]{0:T(1024)(128)(4,1)S(1)}, pred[2048]{0:T(1024)(128)(4,1)}, u32[]{:S(2)}) copy-start(pred[2048]{0:T(1024)(128)(4,1)} %constant.231) | copy-start | bytes 6148
  7.2 30.7 %copy-start.50 = (pred[2048]{0:T(1024)(128)(4,1)S(1)}, pred[2048]{0:T(1024)(128)(4,1)}, u32[]{:S(2)}) copy-start(pred[2048]{0:T(1024)(128)(4,1)} %constant.230) | copy-start | bytes 6148
  7.2 30.6 %copy-start.51 = (pred[2048]{0:T(1024)(128)(4,1)S(1)}, pred[2048]{0:T(1024)(128)(4,1)}, u32[]{:S(2)}) copy-start(pred[2048]{0:T(1024)(128)(4,1)} %constant.229) | copy-start | bytes 6148
  7.2 30.6 %copy-start.52 = (pred[2048]{0:T(1024)(128)(4,1)S(1)}, pred[2048]{0:T(1024)(128)(4,1)}, u32[]{:S(2)}) copy-start(pred[2048]{0:T(1024)(128)(4,1)} %constant.228) | copy-start | bytes 6148
  7.2 30.6 %copy-start.53 = (pred[2048]{0:T(1024)(128)(4,1)S(1)}, pred[2048]{0:T(1024)(128)(4,1)}, u32[]{:S(2)}) copy-start(pred[2048]{0:T(1024)(128)(4,1)} %constant.227) | copy-start | bytes 6148
  7.2 30.6 %copy-start.54 = (pred[2048]{0:T(1024)(128)(4,1)S(1)}, pred[2048]{0:T(1024)(128)(4,1)}, u32[]{:S(2)}) copy-start(pred[2048]{0:T(1024)(128)(4,1)} %constant.226) | copy-start | bytes 6148
  7.3 30.6 %copy-start.55 = (pred[2048]{0:T(1024)(128)(4,1)S(1)}, pred[2048]{0:T(1024)(128)(4,1)}, u32[]{:S(2)}) copy-start(pred[2048]{0:T(1024)(128)(4,1)} %constant.225) | copy-start | bytes 6148
  7.3 41.2 %copy-start.11 = (bf16[512,1536]{1,0:T(8,128)(2,1)S(1)}, bf16[512,1536]{1,0:T(8,128)(2,1)}, u32[]{:S(2)}) copy-start(bf16[512,1536]{1,0:T(8,128)(2,1)} %param.17) | copy-start | bytes 4718596
  7.3 36.5 %copy-start.61 = (bf16[2,64]{1,0:T(2,128)(2,1)S(1)}, bf16[2,64]{1,0:T(2,128)(2,1)}, u32[]{:S(2)}) copy-start(bf16[2,64]{1,0:T(2,128)(2,1)} %param.24) | copy-start | bytes 772
  7.3 63.1 %all-gather.19.cloned.1.call-start = ((), (), s32[]{:S(2)}) async-start(), calls=%async_computation.12 | async-start | bytes 1769472 | tf_op jit(solution)/shard_map/all_gather | solution.py:82
  8.0 72.2 %all-gather.21.cloned.1.call-start = ((), (), s32[]{:S(2)}) async-start(), calls=%async_computation.13 | async-start | bytes 1310720 | tf_op jit(solution)/shard_map/all_gather | solution.py:115
  10.5 59.9 %copy-start.38 = (f32[512]{0:T(512)}, f32[512]{0:T(512)S(1)}, u32[]{:S(2)}) copy-start(f32[512]{0:T(512)S(1)} %get-tuple-element.116) | copy-start | bytes 6148
  37.8 11.6 copy-start.23
  48.4 22.0 %copy-start.34 = (f32[1536]{0:T(1024)}, f32[1536]{0:T(1024)S(1)}, u32[]{:S(2)}) copy-start(f32[1536]{0:T(1024)S(1)} %reshape.300) | copy-start | bytes 18436
  48.5 24.3 %copy-start.18 = (f32[512,128]{0,1:T(8,128)}, f32[512,128]{0,1:T(8,128)S(1)}, u32[]{:S(2)}) copy-start(f32[512,128]{0,1:T(8,128)S(1)} %get-tuple-element.142) | copy-start | bytes 786436
  50.3 59.5 %all-gather.23.cloned.1.call-start = ((), (), s32[]{:S(2)}) async-start(), calls=%async_computation.14 | async-start | bytes 1310720 | tf_op jit(solution)/shard_map/all_gather | solution.py:116
  63.5 9.1 copy-start.24
  65.1 68.5 %all-gather.25.cloned.1.call-start = ((), (), s32[]{:S(2)}) async-start(), calls=%async_computation.15 | async-start | bytes 1769472 | tf_op jit(solution)/shard_map/all_gather | solution.py:88
  65.7 140.4 %all-reduce.13.cloned.1.call-start = ((), (), s32[]{:S(2)}) async-start(), calls=%async_computation.16 | async-start | bytes 6291456 | tf_op jit(solution)/shard_map/psum | solution.py:142
  73.1 15.6 copy-start.29
  86.0 27.3 %copy-start.43 = (f32[512]{0:T(512)}, f32[512]{0:T(512)S(1)}, u32[]{:S(2)}) copy-start(f32[512]{0:T(512)S(1)} %get-tuple-element.131) | copy-start | bytes 6148
  88.7 24.6 %copy-start.44 = (f32[512]{0:T(512)}, f32[512]{0:T(512)S(1)}, u32[]{:S(2)}) copy-start(f32[512]{0:T(512)S(1)} %fusion.1) | copy-start | bytes 6148
  89.7 25.1 %copy-start.41 = (f32[512]{0:T(512)}, f32[512]{0:T(512)S(1)}, u32[]{:S(2)}) copy-start(f32[512]{0:T(512)S(1)} %get-tuple-element.133) | copy-start | bytes 6148
  92.5 22.4 %copy-start.42 = (f32[512]{0:T(512)}, f32[512]{0:T(512)S(1)}, u32[]{:S(2)}) copy-start(f32[512]{0:T(512)S(1)} %fusion) | copy-start | bytes 6148
  109.8 3.9 copy-start.26
  115.9 17.6 copy-start.32
  117.1 20.4 %copy-start.33 = (bf16[512,128]{0,1:T(8,128)(2,1)}, bf16[512,128]{0,1:T(8,128)(2,1)S(1)}, u32[]{:S(2)}) copy-start(bf16[512,128]{0,1:T(8,128)(2,1)S(1)} %fusion.34) | copy-start | bytes 393220
  137.5 157.2 %all-gather.29.cloned.1.call-start = ((), (), s32[]{:S(2)}) async-start(), calls=%async_computation.18 | async-start | bytes 10321920 | tf_op jit(solution)/shard_map/all_gather | solution.py:146
  138.1 245.2 %all-gather.27.cloned.1.call-start = ((), (), s32[]{:S(2)}) async-start(), calls=%async_computation.17 | async-start | bytes 10321920 | tf_op jit(solution)/shard_map/all_gather | solution.py:145
  138.9 333.0 %all-gather.31.cloned.1.call-start = ((), (), s32[]{:S(2)}) async-start(), calls=%async_computation.19 | async-start | bytes 10321920 | tf_op jit(solution)/shard_map/all_gather | solution.py:147
  139.6 426.8 %all-reduce.17.cloned.1.call-start = ((), (), s32[]{:S(2)}) async-start(), calls=%async_computation.21 | async-start | bytes 6291456 | tf_op jit(solution)/shard_map/psum | solution.py:169
  208.9 357.5 %copy-start.10 = (f32[512,1536]{1,0:T(8,128)}, f32[512,1536]{1,0:T(8,128)S(1)}, u32[]{:S(2)}) copy-start(f32[512,1536]{1,0:T(8,128)S(1)} %get-tuple-element.97) | copy-start | bytes 9437188
  471.9 13.3 copy-start.58
  485.2 4.1 copy-start.65
  485.2 4.1 copy-start.21
  497.8 114.4 %all-reduce.15.cloned.1.call-start = ((), (), s32[]{:S(2)}) async-start(), calls=%async_computation.20 | async-start | bytes 3145728 | tf_op jit(solution)/shard_map/psum | solution.py:157
  509.3 199.7 %reduce-scatter.19.cloned.1.call-start = ((), (), s32[]{:S(2)}) async-start(), calls=%async_computation.22 | async-start | bytes 2621440 | tf_op jit(solution)/shard_map/reduce_scatter | solution.py:205
  612.2 6.0 copy-start.20
  620.4 7.2 copy-start.22
  653.6 5.2 copy-start.46
  653.6 5.2 copy-start.47
  653.6 5.2 copy-start.57
  664.9 89.6 %reduce-scatter.21.cloned.1.call-start = ((), (), s32[]{:S(2)}) async-start(), calls=%async_computation.23 | async-start | bytes 2621440 | tf_op jit(solution)/shard_map/reduce_scatter | solution.py:206
  665.4 172.8 %all-reduce.19.cloned.1.call-start = ((), (), s32[]{:S(2)}) async-start(), calls=%async_computation.37 | async-start | bytes 7340032 | tf_op jit(solution)/shard_map/psum | solution.py:212
  665.5 4.6 copy-start.17
  665.5 4.6 copy-start.60
  709.0 261.9 %reduce-scatter.35.cloned.1.call-start = ((), (), s32[]{:S(2)}) async-start(), calls=%async_computation.32 | async-start | bytes 7962624 | tf_op jit(solution)/shard_map/reduce_scatter | solution.py:267
  717.9 385.1 %reduce-scatter.31.cloned.1.call-start = ((), (), s32[]{:S(2)}) async-start(), calls=%async_computation.28 | async-start | bytes 7962624 | tf_op jit(solution)/shard_map/reduce_scatter | solution.py:261
  727.1 507.5 %reduce-scatter.33.cloned.1.call-start = ((), (), s32[]{:S(2)}) async-start(), calls=%async_computation.30 | async-start | bytes 7962624 | tf_op jit(solution)/shard_map/reduce_scatter | solution.py:264
  736.1 4.0 copy-start.35
  736.1 4.0 copy-start.39
  736.1 554.9 %reduce-scatter.37.cloned.1.call-start = ((), (), s32[]{:S(2)}) async-start(), calls=%async_computation.34 | async-start | bytes 36864
  736.9 621.6 %reduce-scatter.29.cloned.1.call-start = ((), (), s32[]{:S(2)}) async-start(), calls=%async_computation.27 | async-start | bytes 1327104 | tf_op jit(solution)/shard_map/reduce_scatter | solution.py:255
  740.0 685.8 %reduce-scatter.23.cloned.1.call-start = ((), (), s32[]{:S(2)}) async-start(), calls=%async_computation.24 | async-start | bytes 1327104 | tf_op jit(solution)/shard_map/reduce_scatter | solution.py:237
  743.8 737.8 %reduce-scatter.41.cloned.1.call-start = ((), (), s32[]{:S(2)}) async-start(), calls=%async_computation.36 | async-start | bytes 36864
  780.2 767.2 %reduce-scatter.27.cloned.1.call-start = ((), (), s32[]{:S(2)}) async-start(), calls=%async_computation.26 | async-start | bytes 884736 | tf_op jit(solution)/shard_map/reduce_scatter | solution.py:249
  783.4 820.8 %reduce-scatter.39.cloned.1.call-start = ((), (), s32[]{:S(2)}) async-start(), calls=%async_computation.35 | async-start | bytes 36864
  841.4 826.9 %reduce-scatter.25.cloned.1.call-start = ((), (), s32[]{:S(2)}) async-start(), calls=%async_computation.25 | async-start | bytes 884736 | tf_op jit(solution)/shard_map/reduce_scatter | solution.py:243
  841.7 392.9 %copy-start.64 = (u32[32]{0:T(128)S(1)}, u32[32]{0:T(128)}, u32[]{:S(2)}) copy-start(u32[32]{0:T(128)} %constant.248) | copy-start | bytes 388
  841.7 394.2 %copy-start.63 = (u32[32]{0:T(128)S(1)}, u32[32]{0:T(128)}, u32[]{:S(2)}) copy-start(u32[32]{0:T(128)} %constant.236) | copy-start | bytes 388
  844.8 895.1 %all-gather.37.cloned.1.call-start = ((), (), s32[]{:S(2)}) async-start(), calls=%async_computation.33 | async-start | bytes 4423680 | tf_op jit(solution)/shard_map/all_gather | solution.py:305
  971.0 839.2 %all-gather.33.cloned.1.call-start = ((), (), s32[]{:S(2)}) async-start(), calls=%async_computation.29 | async-start | bytes 4423680 | tf_op jit(solution)/shard_map/all_gather | solution.py:299
  1103.0 777.3 %all-gather.35.cloned.1.call-start = ((), (), s32[]{:S(2)}) async-start(), calls=%async_computation.31 | async-start | bytes 4423680 | tf_op jit(solution)/shard_map/all_gather | solution.py:302
  1566.6 33.2 %copy-start.45 = (f32[512]{0:T(512)S(1)}, f32[512]{0:T(512)}, u32[]{:S(2)}) copy-start(f32[512]{0:T(512)} %get-tuple-element.115) | copy-start | bytes 6148
  (28 other events, 62.0 us)
Sparse Core Ops, SparseCore 0:
  9.7 32.0 all-gather.18
  50.4 29.7 all-gather.20
  82.4 27.4 all-gather.22
  111.2 22.2 all-gather.24
  137.6 68.4 all-reduce.12
  207.5 87.1 all-gather.28
  296.2 87.0 all-gather.26
  384.8 87.0 all-gather.30
  497.9 68.4 all-reduce.16
  569.2 42.9 all-reduce.14
  665.0 43.9 reduce-scatter.18
  711.3 43.1 reduce-scatter.20
  757.5 80.6 all-reduce.18
  841.8 129.0 reduce-scatter.34
  974.9 128.0 reduce-scatter.30
  1106.5 128.0 reduce-scatter.32
  1238.5 52.5 reduce-scatter.36
  1295.2 63.2 reduce-scatter.28
  1362.8 62.9 reduce-scatter.22
  1429.1 52.4 reduce-scatter.40
  1485.8 61.5 reduce-scatter.26
  1550.5 52.4 reduce-scatter.38
  1606.9 61.4 reduce-scatter.24
  1669.9 69.9 all-gather.36
  1741.6 68.5 all-gather.32
  1811.7 68.5 all-gather.34
where the time goes:
time: 1900 us; the launch traced here: 1890 us
  waiting for transfers between devices  1420 us (75%)
  blocking collectives  200 us (11%)
  matrix products  147 us (8%)
  local copies, waits for them, and re-layouts  54.8 us (3%)
  other arithmetic  52 us (3%)
    reduce_scatter x1, waiting for transfers between devices, local(): lax.psum_scatter(wg_grad.astype(jnp.bfloat16), ('fsdp', 'context'), scatt...  132 us
    reduce_scatter x1, waiting for transfers between devices, local(): lax.psum_scatter(wu_grad.astype(jnp.bfloat16), ('fsdp', 'context'), scatt...  132 us
    reduce_scatter x1, waiting for transfers between devices, local(): lax.psum_scatter(wd_grad.astype(jnp.bfloat16), ('fsdp', 'context'), scatt...  126 us
    unnamed x29, waiting for transfers between devices  95.9 us
    all_gather x1, waiting for transfers between devices, local(): lax.all_gather(w_up, 'fsdp', axis=0, tiled=True)  82.6 us
    all_gather x1, waiting for transfers between devices, local(): lax.all_gather(w_gate, 'fsdp', axis=0, tiled=True)  79.1 us
    all_gather x1, waiting for transfers between devices, local(): lax.all_gather(w_down, 'fsdp', axis=1, tiled=True)  79.1 us
    all_gather x1, waiting for transfers between devices, local(): lax.all_gather(pieces[9].astype(jnp.bfloat16), 'context', axis=0, tiled=T...  64.4 us
  transfers between devices with their start and end apart: 26, of which 24 were waited for; matrix products, arithmetic and copies ran while one was open for 8% of the time, Pallas kernels for 0%

commit v1 on v0

--- a/solution.py
+++ b/solution.py
@@ -10,6 +10,25 @@
 EPSILON = 1e-06
 ROPE_BASE = 1000000.0
 MASKED = -1e30
+
+
+def collect(x, axis, dim):
+    size, index, rows = (lax.axis_size(axis), lax.axis_index(axis), x.shape[dim])
+    ahead = [(i, (i + 1) % size) for i in range(size)]
+    left = [(i, (i - 1) % size) for i in range(size)]
+    out = jnp.zeros((*x.shape[:dim], size * rows, *x.shape[dim + 1 :]), x.dtype)
+    out = lax.dynamic_update_slice_in_dim(out, x, index * rows, axis=dim)
+    from_left = from_right = x
+    halfway = size // 2
+    for hop in range(1, halfway + 1):
+        from_left = lax.ppermute(from_left, axis, ahead)
+        out = lax.dynamic_update_slice_in_dim(out, from_left, (index - hop) % size * rows, axis=dim)
+        if hop < size - halfway:
+            from_right = lax.ppermute(from_right, axis, left)
+            out = lax.dynamic_update_slice_in_dim(
+                out, from_right, (index + hop) % size * rows, axis=dim
+            )
+    return out
 
 
 def rope_tables(positions):
@@ -302,9 +321,7 @@
         lax.all_gather(pieces[10].astype(jnp.bfloat16), "context", axis=0, tiled=True).astype(
             jnp.float32
         ),
-        lax.all_gather(pieces[11].astype(jnp.bfloat16), "context", axis=1, tiled=True).astype(
-            jnp.float32
-        ),
+        collect(pieces[11].astype(jnp.bfloat16), "context", 1).astype(jnp.float32),
     )
     return (
         outputs,

time: 1900 us -> 1840 us (0.968)
  waiting for transfers between devices: 1420 us -> 1290 us
  local copies, waits for them, and re-layouts: 54.8 us -> 103 us
    all_gather x1, waiting for transfers between devices: 64.4 us -> 0.01 us  [local(): lax.all_gather(pieces[9].astype(jnp.bfloat16), 'context', axis=0, tiled=T...]
    all_gather x1 -> x0, waiting for transfers between devices: 54.4 us -> none  [local(): lax.all_gather(pieces[11].astype(jnp.bfloat16), 'context', axis=1, tiled=...]
    dynamic_update_slice x0 -> x4, local copies, waits for them, and re-layouts: none -> 46.5 us  [the longest x2 22.8 us: collect(): lax.dynamic_update_slice_in_dim(out, from_left, (index - hop) % size * ro...]
    unnamed x29 -> x28, waiting for transfers between devices: 95.9 us -> 105 us
    unnamed x152 -> x155, local copies, waits for them, and re-layouts: 43.4 us -> 37.5 us
  transfers between devices with their start and end apart: 26 -> 28, of which waited for: 24 -> 23; matrix products, arithmetic and copies ran while one was open for 8% -> 12% of each run, Pallas kernels for 0% -> 0%
where the time goes in v1:
time: 1840 us; the launch traced here: 1830 us
  waiting for transfers between devices  1290 us (70%)
  blocking collectives  213 us (12%)
  matrix products  148 us (8%)
  local copies, waits for them, and re-layouts  103 us (6%)
  other arithmetic  59.3 us (3%)
    reduce_scatter x1, waiting for transfers between devices, local(): lax.psum_scatter(wu_grad.astype(jnp.bfloat16), ('fsdp', 'context'), scatt...  132 us
    reduce_scatter x1, waiting for transfers between devices, local(): lax.psum_scatter(wg_grad.astype(jnp.bfloat16), ('fsdp', 'context'), scatt...  126 us
    reduce_scatter x1, waiting for transfers between devices, local(): lax.psum_scatter(wd_grad.astype(jnp.bfloat16), ('fsdp', 'context'), scatt...  117 us
    unnamed x28, waiting for transfers between devices  105 us
    all_gather x1, waiting for transfers between devices, local(): lax.all_gather(w_gate, 'fsdp', axis=0, tiled=True)  82.6 us
    all_gather x1, waiting for transfers between devices, local(): lax.all_gather(w_up, 'fsdp', axis=0, tiled=True)  79.1 us
    all_gather x1, waiting for transfers between devices, local(): lax.all_gather(w_down, 'fsdp', axis=1, tiled=True)  79.1 us
    psum x1, waiting for transfers between devices, local(): middle = inputs_f + lax.psum(attn_part, 'tensor')  61.5 us
  transfers between devices with their start and end apart: 28, of which 23 were waited for; matrix products, arithmetic and copies ran while one was open for 12% of the time, Pallas kernels for 0%

profile of v1, /device:TPU:0, one launch (start us, length us, event | category | flops | bytes accessed | tf_op | source)
XLA Modules:
  0.0 1832.6 jit_solution(1100857927830428637)
XLA Ops:
  8.1 13.0 all_gather.78
  21.8 4.4 all-gather
  29.2 5.2 select_select_fusion
  35.1 4.2 all-gather.2
  41.3 4.2 all-gather.3
  45.6 8.7 all_gather.81
  56.6 4.5 all-gather.1
  63.9 7.3 all-gather.20.cloned.1.call-done
  83.4 17.4 all-gather.22.cloned.1.call-done
  108.0 16.5 all-gather.24.cloned.1.call-done
  124.5 3.9 fusion.71
  130.6 4.9 all-gather.4
  135.5 61.5 %all-reduce.13.cloned.1.call-done = f32[512,1536]{1,0:T(8,128)} async-done(((f32[512,1536]{1,0:T(8,128)}), f32[512,1536]{1,0:T(8,128)}) %all-reduce.13.cloned.1.call-update) | async-done | bytes 3145744 | tf_op jit(solution)/shard_map/psum | solution.py:161
  202.9 82.6 %all-gather.26.cloned.1.call-done = bf16[1536,2240]{0,1:T(8,128)(2,1)} async-done(((bf16[768,2240]{0,1:T(8,128)(2,1)}), bf16[1536,2240]{0,1:T(8,128)(2,1)}) %all-gather.26.cloned.1.call-update) | async-done | bytes 6881296 | tf_op jit(solution)/shard_map/all_gather | solution.py:164
  285.6 9.5 fusion.116
  295.1 79.1 %all-gather.28.cloned.1.call-done = bf16[1536,2240]{0,1:T(8,128)(2,1)} async-done(((bf16[768,2240]{0,1:T(8,128)(2,1)}), bf16[1536,2240]{0,1:T(8,128)(2,1)}) %all-gather.28.cloned.1.call-update) | async-done | bytes 6881296 | tf_op jit(solution)/shard_map/all_gather | solution.py:165
  374.2 9.5 fusion.117
  383.7 79.1 %all-gather.30.cloned.1.call-done = bf16[2240,1536]{1,0:T(8,128)(2,1)} async-done(((bf16[2240,768]{1,0:T(8,128)(2,1)}), bf16[2240,1536]{1,0:T(8,128)(2,1)}) %all-gather.30.cloned.1.call-update) | async-done | bytes 6881296 | tf_op jit(solution)/shard_map/all_gather | solution.py:166
  462.8 13.1 multiply_convert_fusion
  475.9 7.9 fusion.118
  483.8 5.6 convolution_add_fusion.2
  493.1 9.3 convolution_convert_fusion.3
  503.8 54.2 %all-reduce.17.cloned.1.call-done = f32[512,1536]{1,0:T(8,128)} async-done(((f32[512,1536]{1,0:T(8,128)}), f32[512,1536]{1,0:T(8,128)}) %all-reduce.17.cloned.1.call-update) | async-done | bytes 3145744 | tf_op jit(solution)/shard_map/psum | solution.py:188
  561.8 41.9 %all-reduce.15.cloned.1.call-done = bf16[512,1536]{1,0:T(8,128)(2,1)} async-done(((bf16[512,1536]{1,0:T(8,128)(2,1)}), bf16[512,1536]{1,0:T(8,128)(2,1)}) %all-reduce.15.cloned.1.call-update) | async-done | bytes 1572880 | tf_op jit(solution)/shard_map/psum | solution.py:176
  603.8 6.0 subtract_add_fusion
  627.6 3.5 multiply_reduce_fusion.1
  638.7 3.5 multiply_reduce_fusion.2
  650.3 6.1 select_add_fusion
  666.5 33.9 %reduce-scatter.19.cloned.1.call-done = f32[512,2,128]{0,2,1:T(8,128)} async-done(((f32[2048,2,128]{0,2,1:T(8,128)}), f32[512,2,128]{0,2,1:T(8,128)}) %reduce-scatter.19.cloned.1.call-update) | async-done | bytes 524304 | tf_op jit(solution)/shard_map/reduce_scatter | solution.py:224
  700.5 8.9 convolution_convert_fusion.2
  709.6 9.0 convolution_convert_fusion.1
  719.5 3.7 convolution_convert_fusion.5
  726.3 19.7 %reduce-scatter.21.cloned.1.call-done = f32[512,2,128]{0,2,1:T(8,128)} async-done(((f32[2048,2,128]{0,2,1:T(8,128)}), f32[512,2,128]{0,2,1:T(8,128)}) %reduce-scatter.21.cloned.1.call-update) | async-done | bytes 524304 | tf_op jit(solution)/shard_map/reduce_scatter | solution.py:225
  746.0 23.9 %all-reduce.20 = bf16[512,2,128]{0,2,1:T(8,128)(2,1)} all-reduce(f32[512,2,128]{0,2,1:T(8,128)} %reduce-scatter.21.cloned.1.call-done), channel_id=1, replica_groups=mesh['fsdp'=2,'context'=4,'tensor'=4] {'tensor'}, use_global_device_ids=true, to_apply=%region_19.20 | all-reduce | flops 131072 | bytes 786432 | tf_op jit(solution)/shard_map/psum | solution.py:231
  774.9 8.8 convolution_convert_fusion
  783.8 45.9 %all-reduce.19.cloned.1.call-done = (f32[512,1536]{1,0:T(8,128)}, f32[512,2,128]{0,2,1:T(8,128)}) async-done(((f32[512,1536]{1,0:T(8,128)}, f32[512,2,128]{0,2,1:T(8,128)}), (f32[512,1536]{1,0:T(8,128)}, f32[512,2,128]{0,2,1:T(8,128)})) %all-reduce.19.cloned.1.call-update) | async-done | bytes 3670032 | tf_op jit(solution)/shard_map/psum | solution.py:231
  836.3 126.1 %reduce-scatter.31.cloned.1.call-done = bf16[192,2240]{1,0:T(8,128)(2,1)} async-done(((bf16[1536,2240]{1,0:T(8,128)(2,1)}), bf16[192,2240]{1,0:T(8,128)(2,1)}) %reduce-scatter.31.cloned.1.call-update) | async-done | bytes 860176 | tf_op jit(solution)/shard_map/reduce_scatter | solution.py:280
  962.5 132.0 %reduce-scatter.33.cloned.1.call-done = bf16[192,2240]{1,0:T(8,128)(2,1)} async-done(((bf16[1536,2240]{1,0:T(8,128)(2,1)}), bf16[192,2240]{1,0:T(8,128)(2,1)}) %reduce-scatter.33.cloned.1.call-update) | async-done | bytes 860176 | tf_op jit(solution)/shard_map/reduce_scatter | solution.py:283
  1097.1 53.5 %reduce-scatter.37.cloned.1.call-done = bf16[16,3]{1,0:T(8,128)(2,1)} async-done(((bf16[128,3]{1,0:T(8,128)(2,1)}), bf16[16,3]{1,0:T(8,128)(2,1)}) %reduce-scatter.37.cloned.1.call-update) | async-done | bytes 112
  1151.4 9.9 all-gather.5
  1162.0 55.6 %reduce-scatter.23.cloned.1.call-done = bf16[192,384]{1,0:T(8,128)(2,1)} async-done(((bf16[1536,384]{1,0:T(8,128)(2,1)}), bf16[192,384]{1,0:T(8,128)(2,1)}) %reduce-scatter.23.cloned.1.call-update) | async-done | bytes 147472 | tf_op jit(solution)/shard_map/reduce_scatter | solution.py:256
  1217.6 17.3 all_gather.90
  1236.0 48.5 %reduce-scatter.29.cloned.1.call-done = bf16[384,192]{0,1:T(8,128)(2,1)} async-done(((bf16[384,1536]{0,1:T(8,128)(2,1)}), bf16[384,192]{0,1:T(8,128)(2,1)}) %reduce-scatter.29.cloned.1.call-update) | async-done | bytes 147472 | tf_op jit(solution)/shard_map/reduce_scatter | solution.py:274
  1284.5 17.5 all_gather.96
  1304.4 35.9 %reduce-scatter.41.cloned.1.call-done = bf16[16,2]{1,0:T(8,128)(2,1)} async-done(((bf16[128,2]{1,0:T(8,128)(2,1)}), bf16[16,2]{1,0:T(8,128)(2,1)}) %reduce-scatter.41.cloned.1.call-update) | async-done | bytes 80
  1341.0 9.8 all-gather.7
  1351.5 54.0 %reduce-scatter.27.cloned.1.call-done = bf16[192,256]{1,0:T(8,128)(2,1)} async-done(((bf16[1536,256]{1,0:T(8,128)(2,1)}), bf16[192,256]{1,0:T(8,128)(2,1)}) %reduce-scatter.27.cloned.1.call-update) | async-done | bytes 98320 | tf_op jit(solution)/shard_map/reduce_scatter | solution.py:268
  1405.5 15.6 all_gather.94
  1422.0 117.0 %reduce-scatter.35.cloned.1.call-done = bf16[2240,192]{0,1:T(8,128)(2,1)} async-done(((bf16[2240,1536]{0,1:T(8,128)(2,1)}), bf16[2240,192]{0,1:T(8,128)(2,1)}) %reduce-scatter.35.cloned.1.call-update) | async-done | bytes 860176 | tf_op jit(solution)/shard_map/reduce_scatter | solution.py:286
  1545.4 28.7 %all-reduce.5 = (bf16[1536]{0:T(1024)(128)(2,1)S(1)}, bf16[1536]{0:T(1024)(128)(2,1)S(1)}) all-reduce(bf16[1536]{0:T(1024)(128)(2,1)S(1)} %get-tuple-element.84, bf16[1536]{0:T(1024)(128)(2,1)S(1)} %copy-done.42), channel_id=4, replica_groups=mesh['fsdp'=2,'context'=4,'tensor'=4] {'fsdp','context'}, use_global_device_ids=true, to_apply=%region_22.23.clone | all-reduce | flops 3072 | bytes 12288
  1574.6 9.4 all-reduce.6
  1587.3 4.4 fusion.12
  1591.7 12.1 reduce-scatter.39.cloned.1.call-done
  1604.5 20.5 %all-gather.6 = bf16[4,16,2]{1,2,0:T(2,128)(2,1)S(1)} all-gather(bf16[1,16,2]{1,2,0:T(2,128)(2,1)S(1)} %bitcast.186), channel_id=1, replica_groups=mesh['fsdp'=2,'context'=4,'tensor'=4] {'context'}, dimensions={0}, use_global_device_ids=true | all-gather | bytes 320 | tf_op jit(solution)/shard_map/all_gather | solution.py:303
  1625.6 52.5 %reduce-scatter.25.cloned.1.call-done = bf16[192,256]{1,0:T(8,128)(2,1)} async-done(((bf16[1536,256]{1,0:T(8,128)(2,1)}), bf16[192,256]{1,0:T(8,128)(2,1)}) %reduce-scatter.25.cloned.1.call-update) | async-done | bytes 98320 | tf_op jit(solution)/shard_map/reduce_scatter | solution.py:262
  1678.2 16.2 all_gather.92
  1699.0 11.2 dynamic_update_slice.12
  1711.9 11.9 dynamic_update_slice.13
  1725.5 12.6 dynamic_update_slice.14
  1739.9 10.9 dynamic_update_slice.15
  1750.7 5.4 convert_element_type.255
  1756.1 6.0 copy.99
  1762.1 57.9 %all-gather.34.cloned.1.call-done = bf16[768,2240]{1,0:T(8,128)(2,1)} async-done(((bf16[192,2240]{1,0:T(8,128)(2,1)}), bf16[768,2240]{1,0:T(8,128)(2,1)}) %all-gather.34.cloned.1.call-update) | async-done | bytes 3440656 | tf_op jit(solution)/shard_map/all_gather | solution.py:321
  1819.9 5.9 copy.100
  (304 shorter events, 137.5 us)
Async XLA Ops:
  7.2 22.0 %copy-start.53 = (pred[2048]{0:T(1024)(128)(4,1)S(1)}, pred[2048]{0:T(1024)(128)(4,1)}, u32[]{:S(2)}) copy-start(pred[2048]{0:T(1024)(128)(4,1)} %constant.252) | copy-start | bytes 6148
  7.2 21.9 %copy-start.54 = (pred[2048]{0:T(1024)(128)(4,1)S(1)}, pred[2048]{0:T(1024)(128)(4,1)}, u32[]{:S(2)}) copy-start(pred[2048]{0:T(1024)(128)(4,1)} %constant.253) | copy-start | bytes 6148
  7.2 21.9 %copy-start.55 = (pred[2048]{0:T(1024)(128)(4,1)S(1)}, pred[2048]{0:T(1024)(128)(4,1)}, u32[]{:S(2)}) copy-start(pred[2048]{0:T(1024)(128)(4,1)} %constant.254) | copy-start | bytes 6148
  7.2 21.9 %copy-start.56 = (pred[2048]{0:T(1024)(128)(4,1)S(1)}, pred[2048]{0:T(1024)(128)(4,1)}, u32[]{:S(2)}) copy-start(pred[2048]{0:T(1024)(128)(4,1)} %constant.255) | copy-start | bytes 6148
  7.2 21.9 %copy-start.57 = (pred[2048]{0:T(1024)(128)(4,1)S(1)}, pred[2048]{0:T(1024)(128)(4,1)}, u32[]{:S(2)}) copy-start(pred[2048]{0:T(1024)(128)(4,1)} %constant.256) | copy-start | bytes 6148
  7.2 21.9 %copy-start.58 = (pred[2048]{0:T(1024)(128)(4,1)S(1)}, pred[2048]{0:T(1024)(128)(4,1)}, u32[]{:S(2)}) copy-start(pred[2048]{0:T(1024)(128)(4,1)} %constant.257) | copy-start | bytes 6148
  7.3 21.9 %copy-start.59 = (pred[2048]{0:T(1024)(128)(4,1)S(1)}, pred[2048]{0:T(1024)(128)(4,1)}, u32[]{:S(2)}) copy-start(pred[2048]{0:T(1024)(128)(4,1)} %constant.258) | copy-start | bytes 6148
  7.3 32.2 %copy-start.11 = (bf16[512,1536]{1,0:T(8,128)(2,1)S(1)}, bf16[512,1536]{1,0:T(8,128)(2,1)}, u32[]{:S(2)}) copy-start(bf16[512,1536]{1,0:T(8,128)(2,1)} %param.17) | copy-start | bytes 4718596
  7.3 21.2 %copy-start.35 = (s32[1,8]{1,0:T(1,128)S(1)}, s32[1,8]{1,0:T(1,128)}, u32[]{:S(2)}) copy-start(s32[1,8]{1,0:T(1,128)} %param.19) | copy-start | bytes 100
  7.3 27.8 %copy-start.63 = (bf16[2,64]{1,0:T(2,128)(2,1)S(1)}, bf16[2,64]{1,0:T(2,128)(2,1)}, u32[]{:S(2)}) copy-start(bf16[2,64]{1,0:T(2,128)(2,1)} %param.24) | copy-start | bytes 772
  7.3 53.9 %all-gather.18.cloned.1.call-start = ((), (), s32[]{:S(2)}) async-start(), calls=%async_computation.12 | async-start | bytes 1769472 | tf_op jit(solution)/shard_map/all_gather | solution.py:101
  8.0 63.1 %all-gather.20.cloned.1.call-start = ((), (), s32[]{:S(2)}) async-start(), calls=%async_computation.13 | async-start | bytes 1310720 | tf_op jit(solution)/shard_map/all_gather | solution.py:134
  21.1 19.2 %copy-start.24 = (bf16[1536,256]{1,0:T(8,128)(2,1)}, bf16[1536,256]{1,0:T(8,128)(2,1)S(1)}, u32[]{:S(2)}) copy-start(bf16[1536,256]{1,0:T(8,128)(2,1)S(1)} %all_gather.78) | copy-start | bytes 2359300
  28.5 32.7 %copy-start.40 = (f32[512]{0:T(512)}, f32[512]{0:T(512)S(1)}, u32[]{:S(2)}) copy-start(f32[512]{0:T(512)S(1)} %get-tuple-element.116) | copy-start | bytes 6148
  39.4 24.2 %copy-start.19 = (f32[512,128]{0,1:T(8,128)}, f32[512,128]{0,1:T(8,128)S(1)}, u32[]{:S(2)}) copy-start(f32[512,128]{0,1:T(8,128)S(1)} %get-tuple-element.142) | copy-start | bytes 786436
  41.3 59.5 %all-gather.22.cloned.1.call-start = ((), (), s32[]{:S(2)}) async-start(), calls=%async_computation.14 | async-start | bytes 1310720 | tf_op jit(solution)/shard_map/all_gather | solution.py:135
  54.3 9.1 copy-start.25
  55.9 68.6 %all-gather.24.cloned.1.call-start = ((), (), s32[]{:S(2)}) async-start(), calls=%async_computation.15 | async-start | bytes 1769472 | tf_op jit(solution)/shard_map/all_gather | solution.py:107
  56.5 140.6 %all-reduce.13.cloned.1.call-start = ((), (), s32[]{:S(2)}) async-start(), calls=%async_computation.16 | async-start | bytes 6291456 | tf_op jit(solution)/shard_map/psum | solution.py:161
  63.9 15.8 copy-start.30
  73.2 27.6 %copy-start.45 = (f32[512]{0:T(512)}, f32[512]{0:T(512)S(1)}, u32[]{:S(2)}) copy-start(f32[512]{0:T(512)S(1)} %get-tuple-element.129) | copy-start | bytes 6148
  75.9 24.9 %copy-start.46 = (f32[512]{0:T(512)}, f32[512]{0:T(512)S(1)}, u32[]{:S(2)}) copy-start(f32[512]{0:T(512)S(1)} %fusion.2) | copy-start | bytes 6148
  76.9 27.3 %copy-start.47 = (f32[512]{0:T(512)}, f32[512]{0:T(512)S(1)}, u32[]{:S(2)}) copy-start(f32[512]{0:T(512)S(1)} %get-tuple-element.131) | copy-start | bytes 6148
  79.6 24.6 %copy-start.48 = (f32[512]{0:T(512)}, f32[512]{0:T(512)S(1)}, u32[]{:S(2)}) copy-start(f32[512]{0:T(512)S(1)} %fusion.1) | copy-start | bytes 6148
  80.6 25.2 %copy-start.43 = (f32[512]{0:T(512)}, f32[512]{0:T(512)S(1)}, u32[]{:S(2)}) copy-start(f32[512]{0:T(512)S(1)} %get-tuple-element.133) | copy-start | bytes 6148
  83.4 22.4 %copy-start.44 = (f32[512]{0:T(512)}, f32[512]{0:T(512)S(1)}, u32[]{:S(2)}) copy-start(f32[512]{0:T(512)S(1)} %fusion) | copy-start | bytes 6148
  106.9 17.6 copy-start.33
  108.0 20.4 %copy-start.34 = (bf16[512,128]{0,1:T(8,128)(2,1)}, bf16[512,128]{0,1:T(8,128)(2,1)S(1)}, u32[]{:S(2)}) copy-start(bf16[512,128]{0,1:T(8,128)(2,1)S(1)} %fusion.34) | copy-start | bytes 393220
  128.4 157.2 %all-gather.26.cloned.1.call-start = ((), (), s32[]{:S(2)}) async-start(), calls=%async_computation.17 | async-start | bytes 10321920 | tf_op jit(solution)/shard_map/all_gather | solution.py:164
  129.0 245.2 %all-gather.28.cloned.1.call-start = ((), (), s32[]{:S(2)}) async-start(), calls=%async_computation.18 | async-start | bytes 10321920 | tf_op jit(solution)/shard_map/all_gather | solution.py:165
  129.8 333.0 %all-gather.30.cloned.1.call-start = ((), (), s32[]{:S(2)}) async-start(), calls=%async_computation.19 | async-start | bytes 10321920 | tf_op jit(solution)/shard_map/all_gather | solution.py:166
  130.5 427.5 %all-reduce.17.cloned.1.call-start = ((), (), s32[]{:S(2)}) async-start(), calls=%async_computation.21 | async-start | bytes 6291456 | tf_op jit(solution)/shard_map/psum | solution.py:188
  199.9 358.1 %copy-start.10 = (f32[512,1536]{1,0:T(8,128)}, f32[512,1536]{1,0:T(8,128)S(1)}, u32[]{:S(2)}) copy-start(f32[512,1536]{1,0:T(8,128)S(1)} %get-tuple-element.97) | copy-start | bytes 9437188
  475.9 7.9 copy-start.67
  475.9 7.9 copy-start.22
  475.9 7.9 copy-start.18
  489.4 114.4 %all-reduce.15.cloned.1.call-start = ((), (), s32[]{:S(2)}) async-start(), calls=%async_computation.20 | async-start | bytes 3145728 | tf_op jit(solution)/shard_map/psum | solution.py:176
  502.3 198.1 %reduce-scatter.19.cloned.1.call-start = ((), (), s32[]{:S(2)}) async-start(), calls=%async_computation.22 | async-start | bytes 2621440 | tf_op jit(solution)/shard_map/reduce_scatter | solution.py:224
  603.8 6.0 copy-start.21
  612.0 7.2 copy-start.23
  645.0 5.2 copy-start.50
  645.1 5.2 copy-start.51
  656.4 89.6 %reduce-scatter.21.cloned.1.call-start = ((), (), s32[]{:S(2)}) async-start(), calls=%async_computation.23 | async-start | bytes 2621440 | tf_op jit(solution)/shard_map/reduce_scatter | solution.py:225
  657.0 172.8 %all-reduce.19.cloned.1.call-start = ((), (), s32[]{:S(2)}) async-start(), calls=%async_computation.36 | async-start | bytes 7340032 | tf_op jit(solution)/shard_map/psum | solution.py:231
  657.0 4.6 copy-start.17
  657.0 4.6 copy-start.62
  700.4 262.0 %reduce-scatter.31.cloned.1.call-start = ((), (), s32[]{:S(2)}) async-start(), calls=%async_computation.28 | async-start | bytes 7962624 | tf_op jit(solution)/shard_map/reduce_scatter | solution.py:280
  709.4 385.2 %reduce-scatter.33.cloned.1.call-start = ((), (), s32[]{:S(2)}) async-start(), calls=%async_computation.30 | async-start | bytes 7962624 | tf_op jit(solution)/shard_map/reduce_scatter | solution.py:283
  718.6 432.1 %reduce-scatter.37.cloned.1.call-start = ((), (), s32[]{:S(2)}) async-start(), calls=%async_computation.33 | async-start | bytes 36864
  719.4 498.2 %reduce-scatter.23.cloned.1.call-start = ((), (), s32[]{:S(2)}) async-start(), calls=%async_computation.24 | async-start | bytes 1327104 | tf_op jit(solution)/shard_map/reduce_scatter | solution.py:256
  723.2 561.4 %reduce-scatter.29.cloned.1.call-start = ((), (), s32[]{:S(2)}) async-start(), calls=%async_computation.27 | async-start | bytes 1327104 | tf_op jit(solution)/shard_map/reduce_scatter | solution.py:274
  726.3 614.0 %reduce-scatter.41.cloned.1.call-start = ((), (), s32[]{:S(2)}) async-start(), calls=%async_computation.35 | async-start | bytes 36864
  771.7 633.8 %reduce-scatter.27.cloned.1.call-start = ((), (), s32[]{:S(2)}) async-start(), calls=%async_computation.26 | async-start | bytes 884736 | tf_op jit(solution)/shard_map/reduce_scatter | solution.py:268
  774.9 764.1 %reduce-scatter.35.cloned.1.call-start = ((), (), s32[]{:S(2)}) async-start(), calls=%async_computation.32 | async-start | bytes 7962624 | tf_op jit(solution)/shard_map/reduce_scatter | solution.py:286
  783.8 819.9 %reduce-scatter.39.cloned.1.call-start = ((), (), s32[]{:S(2)}) async-start(), calls=%async_computation.34 | async-start | bytes 36864
  832.9 845.3 %reduce-scatter.25.cloned.1.call-start = ((), (), s32[]{:S(2)}) async-start(), calls=%async_computation.25 | async-start | bytes 884736 | tf_op jit(solution)/shard_map/reduce_scatter | solution.py:262
  833.2 261.5 %copy-start.66 = (u32[32]{0:T(128)S(1)}, u32[32]{0:T(128)}, u32[]{:S(2)}) copy-start(u32[32]{0:T(128)} %constant.275) | copy-start | bytes 388
  833.2 262.7 %copy-start.65 = (u32[32]{0:T(128)S(1)}, u32[32]{0:T(128)}, u32[]{:S(2)}) copy-start(u32[32]{0:T(128)} %constant.263) | copy-start | bytes 388
  836.3 919.8 %all-gather.32.cloned.1.call-start = ((), (), s32[]{:S(2)}) async-start(), calls=%async_computation.29 | async-start | bytes 4423680 | tf_op jit(solution)/shard_map/all_gather | solution.py:318
  962.5 857.5 %all-gather.34.cloned.1.call-start = ((), (), s32[]{:S(2)}) async-start(), calls=%async_computation.31 | async-start | bytes 4423680 | tf_op jit(solution)/shard_map/all_gather | solution.py:321
  1539.0 47.2 %collective-permute-start = (bf16[2240,192]{0,1:T(8,128)(2,1)}, bf16[2240,192]{0,1:T(8,128)(2,1)}, u32[]{:S(2)}, u32[]{:S(2)}) collective-permute-start(bf16[2240,192]{0,1:T(8,128)(2,1)} %reduce-scatter.35.cloned.1.call-done), channel_id=1, source_target_pairs={{0,4},{4,8},{8,12},{12,0},{1,5},{5,9},{9,13},{13,1},{2,6},{6,10},{... | collective-permute-start | bytes 2580488 | tf_op jit(solution)/shard_map/ppermute | solution.py:24
  1542.5 44.8 %copy-start.49 = (f32[512]{0:T(512)S(1)}, f32[512]{0:T(512)}, u32[]{:S(2)}) copy-start(f32[512]{0:T(512)} %get-tuple-element.115) | copy-start | bytes 6148
  1585.2 138.5 %collective-permute-start.1 = (bf16[2240,192]{0,1:T(8,128)(2,1)}, bf16[2240,192]{0,1:T(8,128)(2,1)}, u32[]{:S(2)}, u32[]{:S(2)}) collective-permute-start(bf16[2240,192]{0,1:T(8,128)(2,1)} %reduce-scatter.35.cloned.1.call-done), channel_id=1, source_target_pairs={{0,12},{4,0},{8,4},{12,8},{1,13},{5,1},{9,5},{13,9},{2,14},{6,2},{... | collective-permute-start | bytes 2580488 | tf_op jit(solution)/shard_map/ppermute | solution.py:27
  1586.2 151.9 %collective-permute-start.2 = (bf16[2240,192]{0,1:T(8,128)(2,1)}, bf16[2240,192]{0,1:T(8,128)(2,1)}, u32[]{:S(2)}, u32[]{:S(2)}) collective-permute-start(bf16[2240,192]{0,1:T(8,128)(2,1)} %collective-permute-done), channel_id=1, source_target_pairs={{0,4},{4,8},{8,12},{12,0},{1,5},{5,9},{9,13},{13,1},{2,6},{6,10},{... | collective-permute-start | bytes 2580488 | tf_op jit(solution)/shard_map/ppermute | solution.py:24
  (32 other events, 71.6 us)
Sparse Core Ops, SparseCore 0:
  9.7 25.5 all-gather.17
  41.4 29.7 all-gather.19
  73.3 27.4 all-gather.21
  102.2 22.2 all-gather.23
  128.6 68.4 all-reduce.12
  198.4 87.1 all-gather.25
  287.1 87.0 all-gather.27
  375.7 87.0 all-gather.29
  489.5 68.4 all-reduce.16
  560.8 42.9 all-reduce.14
  656.5 43.8 reduce-scatter.18
  702.7 43.2 reduce-scatter.20
  749.1 80.6 all-reduce.18
  833.3 129.1 reduce-scatter.30
  966.4 128.0 reduce-scatter.32
  1098.1 52.5 reduce-scatter.36
  1154.5 63.0 reduce-scatter.22
  1221.4 63.0 reduce-scatter.28
  1287.7 52.5 reduce-scatter.40
  1343.9 61.5 reduce-scatter.26
  1409.7 129.3 reduce-scatter.34
  1542.1 61.5 reduce-scatter.38
  1607.6 70.5 reduce-scatter.24
  1679.7 69.9 all-gather.31
  1751.3 68.5 all-gather.33
